TPU v7x, 32 devices: a whole 2x2x4 slice. The times are simulated.
32 devices in a mesh: tm: 4 (over y, x), pair: 8 (over z, core).
Axes of the slice: x: 2, y: 2, z: 4, core: 2. Of those that a mesh axis runs over, the one named last changes fastest.
Arguments:
- three_center: bfloat16 [192, 64, 1024], P('pair'), may hold values from -6 to 6
- green_occ: bfloat16 [4, 64, 64, 64], P('tm'), may hold values from -0.75 to 0.75
- green_vir: bfloat16 [4, 64, 64, 64], P('tm'), may hold values from -0.75 to 0.75
- pair_list: int32 [192], P('pair'), may hold values from 0 to 63
- block_counts: int32 [8], P('pair'), may hold values from 6 to 24, as said below
- cosine_weights: float32 [4, 4], replicated, may hold values from -3 to 3
- coulomb_rows: int32 [8, 3], replicated, may hold values from 0 to 7, as said below
- coulomb_blocks: float32 [8, 3, 128, 128], replicated, may hold values from -0.3125 to 0.3125
Outputs:
- screened: float32 [4, 1024, 1024], P('tm', 'pair')
Inputs may be any that keep to these rules, and one draw needn't show every extreme that they name: `block_counts`: slots from the count on are not used; some index of pair has all 24 slots live. `coulomb_rows`: the row blocks of one column block are distinct, and the first is the column block itself.
All inputs are finite; a program needn't handle non-finite values.
Results may differ from a plain program's by a relative error of at most 0.0041.
Values sent between devices are 32-bit elements; how exact they have to be, the bound alone decides.
A program may use at most 64 MiB of HBM per device.

v0:
```python
import math
import jax
import jax.numpy as jnp
from jax import lax
from jax.sharding import PartitionSpec as P


def half_product(green_matrix, pair_list, alive_mask, three_center):
    picked = green_matrix[0][pair_list]
    product = jnp.einsum("bij,bjp->bip", picked, three_center, preferred_element_type=jnp.float32)
    product = product * alive_mask[:, None, None]
    return product.astype(jnp.bfloat16).reshape(-1, three_center.shape[2])


def local(
    three_center,
    green_occ,
    green_vir,
    pair_list,
    block_counts,
    cosine_weights,
    coulomb_rows,
    coulomb_blocks,
):
    slots = three_center.shape[0]
    pair_devices = lax.axis_size("pair")
    alive_mask = (jnp.arange(slots, dtype=jnp.int32) < block_counts[0]).astype(jnp.float32)
    left_side = half_product(green_occ, pair_list, alive_mask, three_center)
    right_side = half_product(green_vir, pair_list, alive_mask, three_center)
    normalizer = 1.0 / math.sqrt(slots * three_center.shape[1] * pair_devices)
    summed = lax.dot_general(
        left_side, right_side, (((0,), (0,)), ((), ())), preferred_element_type=jnp.float32
    )
    row_slab = lax.psum_scatter(summed * normalizer, "pair", scatter_dimension=0, tiled=True)
    transformed = jnp.einsum(
        "ft,trc->frc",
        cosine_weights,
        lax.all_to_all(row_slab[None], "tm", split_axis=2, concat_axis=0, tiled=True),
        precision=lax.Precision.HIGHEST,
    )
    spectra = lax.all_to_all(transformed, "tm", split_axis=0, concat_axis=2, tiled=True)
    rows_here = spectra.shape[1]
    column_blocks = coulomb_rows.shape[0]
    per_column = coulomb_rows.shape[1]
    block_width = coulomb_blocks.shape[2]
    blocked = spectra.reshape(rows_here, column_blocks, block_width)
    gathered = jnp.take(blocked, coulomb_rows.reshape(-1), axis=1)
    factors = coulomb_blocks.reshape(column_blocks * per_column, block_width, block_width)
    screened = jnp.einsum("mjx,jxy->mjy", gathered, factors, precision=lax.Precision.HIGHEST)
    screened = screened.reshape(rows_here, column_blocks, per_column, block_width).sum(axis=2)
    return screened.reshape(1, rows_here, column_blocks * block_width)


def solution(mesh):
    return jax.shard_map(
        local,
        mesh=mesh,
        in_specs=(
            P("pair", None, None),
            P("tm", None, None, None),
            P("tm", None, None, None),
            P("pair"),
            P("pair"),
            P(),
            P(),
            P(),
        ),
        out_specs=P("tm", "pair", None),
        check_vma=False,
    )
```

profile of v0, /device:TPU:16, one launch (start us, length us, event | category | flops | bytes accessed | tf_op | source)
XLA Modules:
  0.0 127.4 jit_solution(750855462552319083)
XLA Ops:
  6.5 0.0 copy-start
  6.5 0.0 reduce-scatter.2.cloned.1.call-start
  6.5 0.8 compare_select_fusion.1
  7.4 2.0 %gather_fusion = bf16[24,64,64]{2,1,0:T(8,128)(2,1)S(1)} fusion(bf16[64,64,64]{2,1,0:T(8,128)(2,1)} %bitcast.43, s32[1024]{0:T(1024)S(1)} %pad_clamp_fusion.1), kind=kCustom, calls=%fused_computation | custom fusion | bytes 393312 | tf_op jit(solution)/shard_map/gather | solution.py:9
  9.3 2.6 %gather_fusion.1 = bf16[24,64,64]{2,1,0:T(8,128)(2,1)} fusion(bf16[64,64,64]{2,1,0:T(8,128)(2,1)} %bitcast.44, s32[1024]{0:T(1024)S(1)} %pad_clamp_fusion.1), kind=kCustom, calls=%fused_computation.1 | custom fusion | bytes 393312 | tf_op jit(solution)/shard_map/gather | solution.py:9
  12.6 0.0 copy-done
  12.6 8.2 %bitcast_multiply_fusion = f32[1024,1024]{1,0:T(8,128)} fusion(f32[24]{0:T(128)S(1)} %compare_convert_fusion, bf16[24,64,64]{2,1,0:T(8,128)(2,1)} %gather_fusion.1, bf16[24,64,1024]{2,1,0:T(8,128)(2,1)S(1)} %copy-done, bf16[24,64,64]{2,1,0:T(8,128)(2,1)S(1)} %gather_fusion), kind=kOutput, calls=%fused_computation.5 | convolution fusion | flops 3631218688 | bytes 7733344 | tf_op jit(solution)/shard_map/dot_general | solution.py:31
  20.8 0.0 copy-start.2
  20.8 0.0 copy-start.1
  20.8 0.0 reduce-scatter.2.cloned.1.call-update
  20.9 48.7 %reduce-scatter.2.cloned.1.call-done = f32[128,1024]{1,0:T(8,128)} async-done(((f32[1024,1024]{1,0:T(8,128)}), f32[128,1024]{1,0:T(8,128)}) %reduce-scatter.2.cloned.1.call-update) | async-done | bytes 524304 | tf_op jit(solution)/shard_map/reduce_scatter | solution.py:34
  69.6 1.9 %copy.20 = f32[1,128,1024]{1,0,2:T(1,128)} copy(f32[1,128,1024]{2,1,0:T(8,128)} %bitcast.42) | data formatting | bytes 1048576 | tf_op jit(solution)/shard_map/broadcast_in_dim | solution.py:38
  71.5 4.1 %all-to-all-start = ((f32[1,128,1024]{1,0,2:T(1,128)}), f32[1,128,1024]{1,0,2:T(1,128)}, u32[]{:S(2)}, u32[]{:S(2)}) async-start(f32[1,128,1024]{1,0,2:T(1,128)} %copy.20), calls=%async_computation.1 | async-start | bytes 1048576 | tf_op jit(solution)/shard_map/all_to_all | solution.py:38
  75.6 0.0 copy-done.2
  75.6 0.1 copy.19
  75.7 0.1 reshape.61
  75.8 9.1 %all-to-all-done = f32[1,128,1024]{1,0,2:T(1,128)} async-done(((f32[1,128,1024]{1,0,2:T(1,128)}), f32[1,128,1024]{1,0,2:T(1,128)}, u32[]{:S(2)}, u32[]{:S(2)}) %all-to-all-start) | async-done | bytes 524320 | tf_op jit(solution)/shard_map/all_to_all | solution.py:38
  84.9 2.0 %copy.28 = f32[1,128,4,256]{3,2,1,0:T(4,128)} copy(f32[1,128,4,256]{1,3,2,0:T(8,128)} %bitcast.5) | data formatting | bytes 1048576 | tf_op jit(solution)/shard_map/all_to_all | solution.py:38
  87.0 0.0 copy-done.1
  87.0 2.0 %convolution_bitcast_fusion = f32[4,128,256]{2,0,1:T(4,128)S(1)} fusion(f32[1,128,4,256]{3,2,1,0:T(4,128)} %copy.28, f32[4,4]{1,0:T(4,128)S(1)} %copy-done.1), kind=kOutput, calls=%fused_computation.13 | convolution fusion | flops 6291456 | bytes 1048640 | tf_op jit(solution)/shard_map/ft,trc->frc/dot_general | solution.py:35
  89.0 0.9 copy.22
  89.9 4.1 %all-to-all-start.1 = ((f32[4,128,256]{2,1,0:T(8,128)}), f32[4,128,256]{2,1,0:T(8,128)}, u32[]{:S(2)}, u32[]{:S(2)}) async-start(f32[4,128,256]{2,1,0:T(8,128)} %copy.22), calls=%async_computation.2 | async-start | bytes 1048576 | tf_op jit(solution)/shard_map/all_to_all | solution.py:41
  94.1 0.1 reshape.59
  94.2 8.3 %all-to-all-done.1 = f32[4,128,256]{2,1,0:T(8,128)} async-done(((f32[4,128,256]{2,1,0:T(8,128)}), f32[4,128,256]{2,1,0:T(8,128)}, u32[]{:S(2)}, u32[]{:S(2)}) %all-to-all-start.1) | async-done | bytes 524320 | tf_op jit(solution)/shard_map/all_to_all | solution.py:41
  102.5 2.0 %copy.23 = f32[4,128,256]{1,2,0:T(8,128)} copy(f32[4,128,256]{2,1,0:T(8,128)} %all-to-all-done.1) | data formatting | bytes 1048576 | tf_op jit(solution)/shard_map/all_to_all | solution.py:41
  104.5 2.0 %copy.25 = f32[128,8,128]{2,0,1:T(8,128)} copy(f32[128,8,128]{0,2,1:T(8,128)} %bitcast.39) | data formatting | bytes 1048576 | tf_op jit(solution)/shard_map/reshape | solution.py:46
  106.5 2.9 %gather_fusion.2 = f32[24,128,128]{2,1,0:T(8,128)} fusion(f32[128,8,128]{2,0,1:T(8,128)} %copy.25, s32[1024]{0:T(1024)S(1)} %pad_clamp_fusion), kind=kCustom, calls=%fused_computation.2 | custom fusion | bytes 3145824 | tf_op jit(solution)/shard_map/jit(_take)/gather | solution.py:47
  109.4 4.8 %fusion.6 = f32[24,128,128]{2,1,0:T(8,128)} fusion(f32[24,128,128]{2,1,0:T(8,128)} %bitcast.41, f32[24,128,128]{2,1,0:T(8,128)} %gather_fusion.2, pred[24]{0:T(512)(128)(4,1)S(1)} %compare_and_fusion), kind=kOutput, calls=%fused_computation.10 | convolution fusion | flops 604372992 | bytes 4718616 | tf_op jit(solution)/shard_map/mjx,jxy->mjy/dot_general | solution.py:49
  114.1 2.3 %reduce_sum.9 = f32[128,8,128]{2,0,1:T(8,128)} reduce(f32[128,8,3,128]{3,0,2,1:T(8,128)} %bitcast.38, f32[]{:T(128)} %constant.22.clone.1), dimensions={2}, to_apply=%region_1.2 | reduce | flops 262144 | bytes 2097156 | tf_op jit(solution)/shard_map/reduce_sum | solution.py:50
  116.5 2.0 %copy.26 = f32[128,8,128]{0,2,1:T(8,128)} copy(f32[128,8,128]{2,0,1:T(8,128)} %reduce_sum.9) | data formatting | bytes 1048576 | tf_op jit(solution)/shard_map/reduce_sum | solution.py:50
  118.5 2.0 %copy.27 = f32[1,128,1024]{2,1,0:T(8,128)} copy(f32[1,128,1024]{1,2,0:T(8,128)} %bitcast.40) | data formatting | bytes 1048576 | tf_op jit(solution)/shard_map/reshape | solution.py:51
  (5 shorter events, 0.0 us)
Async XLA Ops:
  6.5 6.1 %copy-start = (bf16[24,64,1024]{2,1,0:T(8,128)(2,1)S(1)}, bf16[24,64,1024]{2,1,0:T(8,128)(2,1)}, u32[]{:S(2)}) copy-start(bf16[24,64,1024]{2,1,0:T(8,128)(2,1)} %param.8) | copy-start | bytes 9437188
  6.5 63.0 %reduce-scatter.2.cloned.1.call-start = ((), (), s32[]{:S(2)}) async-start(), calls=%async_computation.3 | async-start | bytes 4718592 | tf_op jit(solution)/shard_map/reduce_scatter | solution.py:34
  20.8 54.8 %copy-start.2 = (s32[8,3]{0,1:T(4,128)S(1)}, s32[8,3]{0,1:T(4,128)}, u32[]{:S(2)}) copy-start(s32[8,3]{0,1:T(4,128)} %param.14) | copy-start | bytes 292
  20.8 66.1 %copy-start.1 = (f32[4,4]{1,0:T(4,128)S(1)}, f32[4,4]{1,0:T(4,128)}, u32[]{:S(2)}) copy-start(f32[4,4]{1,0:T(4,128)} %param.13) | copy-start | bytes 196
  71.5 13.4 %all-to-all-start = ((f32[1,128,1024]{1,0,2:T(1,128)}), f32[1,128,1024]{1,0,2:T(1,128)}, u32[]{:S(2)}, u32[]{:S(2)}) async-start(f32[1,128,1024]{1,0,2:T(1,128)} %copy.20), calls=%async_computation.1 | async-start | bytes 1048576 | tf_op jit(solution)/shard_map/all_to_all | solution.py:38
  89.9 12.6 %all-to-all-start.1 = ((f32[4,128,256]{2,1,0:T(8,128)}), f32[4,128,256]{2,1,0:T(8,128)}, u32[]{:S(2)}, u32[]{:S(2)}) async-start(f32[4,128,256]{2,1,0:T(8,128)} %copy.22), calls=%async_computation.2 | async-start | bytes 1048576 | tf_op jit(solution)/shard_map/all_to_all | solution.py:41
Sparse Core Ops, SparseCore 0:
  21.0 48.5 reduce-scatter.1
where the time goes:
time: 128 us; the launch traced here: 127 us
  waiting for transfers between devices  66.1 us (52%)
  local copies, waits for them, and re-layouts  20.7 us (16%)
  matrix products  15.1 us (12%)
  between operations  14.1 us (11%)
  starting transfers between devices  8.29 us (6%)
  other arithmetic  3.18 us (2%)
    reduce_scatter x1, waiting for transfers between devices, local(): lax.psum_scatter(summed * normalizer, 'pair', scatter_dimension=0, tiled=...  48.7 us
    all_to_all x1, waiting for transfers between devices, local(): lax.all_to_all(row_slab[None], 'tm', split_axis=2, concat_axis=0, tiled=T...  9.1 us
    all_to_all x1, waiting for transfers between devices, local(): lax.all_to_all(transformed, 'tm', split_axis=0, concat_axis=2, tiled=True)  8.31 us
    dot_general x1, matrix products, local(): lax.dot_general(left_side, right_side, (((0,), (0,)), ((), ())), preferre...  8.24 us
    dot_general x1, matrix products, local(): jnp.einsum('mjx,jxy->mjy', gathered, factors, precision=lax.Precision.HIG...  4.76 us
    gather x2, local copies, waits for them, and re-layouts, half_product(): picked = green_matrix[0][pair_list]  4.56 us
    all_to_all x1, starting transfers between devices, local(): lax.all_to_all(row_slab[None], 'tm', split_axis=2, concat_axis=0, tiled=T...  4.14 us
    all_to_all x1, starting transfers between devices, local(): lax.all_to_all(transformed, 'tm', split_axis=0, concat_axis=2, tiled=True)  4.14 us
  transfers between devices with their start and end apart: 3, of which 3 were waited for; matrix products, arithmetic and copies ran while one was open for 0% of the time, Pallas kernels for 0%

commit v1 on v0

--- a/solution.py
+++ b/solution.py
@@ -3,6 +3,18 @@
 import jax.numpy as jnp
 from jax import lax
 from jax.sharding import PartitionSpec as P
+
+
+def split_up(x, dim, devices):
+    shape = x.shape
+    tiles = x.reshape(*shape[:dim], devices, shape[dim] // devices, *shape[dim + 1 :])
+    return jnp.moveaxis(tiles, dim, 0)
+
+
+def laid_out(blocks, dim):
+    blocks = jnp.moveaxis(blocks, 0, dim)
+    lengths = blocks.shape
+    return blocks.reshape(*lengths[:dim], lengths[dim] * lengths[dim + 1], *lengths[dim + 2 :])
 
 
 def half_product(green_matrix, pair_list, alive_mask, three_center):
@@ -38,7 +50,14 @@
         lax.all_to_all(row_slab[None], "tm", split_axis=2, concat_axis=0, tiled=True),
         precision=lax.Precision.HIGHEST,
     )
-    spectra = lax.all_to_all(transformed, "tm", split_axis=0, concat_axis=2, tiled=True)
+    devices, index = (lax.axis_size("tm"), lax.axis_index("tm"))
+    pieces = split_up(transformed, 0, devices)
+    done = [pieces[index]]
+    for step in range(1, devices):
+        sent = pieces[(index + step) % devices]
+        done.append(lax.ppermute(sent, "tm", [(i, (i + step) % devices) for i in range(devices)]))
+    pieces = jnp.stack(done)[(index - jnp.arange(devices)) % devices]
+    spectra = laid_out(pieces, 2)
     rows_here = spectra.shape[1]
     column_blocks = coulomb_rows.shape[0]
     per_column = coulomb_rows.shape[1]

time: 128 us -> 129 us (level)
  waiting for transfers between devices: 66.1 us -> 62.8 us
  local copies, waits for them, and re-layouts: 20.7 us -> 23.1 us
    all_to_all x1 -> x0, waiting for transfers between devices: 8.31 us -> none  [local(): lax.all_to_all(transformed, 'tm', split_axis=0, concat_axis=2, tiled=True)]
    ppermute x0 -> x3, waiting for transfers between devices: none -> 5.67 us  [local(): lax.ppermute(sent, 'tm', [(i, (i + step) % devices) for i in range(device...]
    all_to_all x1 -> x0, starting transfers between devices: 4.14 us -> none  [local(): lax.all_to_all(transformed, 'tm', split_axis=0, concat_axis=2, tiled=True)]
    ppermute x0 -> x3, starting transfers between devices: none -> 3.67 us  [local(): lax.ppermute(sent, 'tm', [(i, (i + step) % devices) for i in range(device...]
    another operation x0 -> x2, local copies, waits for them, and re-layouts: none -> 2.5 us  [the longest x1 2.04 us: local(): blocked = spectra.reshape(rows_here, column_blocks, block_width)]
    gather x0 -> x1, local copies, waits for them, and re-layouts: none -> 2.41 us  [local(): pieces = jnp.stack(done)[(index - jnp.arange(devices)) % devices]]
    all_to_all x1 -> x0, local copies, waits for them, and re-layouts: 2.04 us -> none  [local(): lax.all_to_all(transformed, 'tm', split_axis=0, concat_axis=2, tiled=True)]
    transpose x0 -> x1, local copies, waits for them, and re-layouts: none -> 2.03 us  [laid_out(): blocks = jnp.moveaxis(blocks, 0, dim)]
  transfers between devices with their start and end apart: 3 -> 5, of which waited for: 3 -> 4; matrix products, arithmetic and copies ran while one was open for 0% -> 0% of each run, Pallas kernels for 0% -> 0%
where the time goes in v1:
time: 129 us; the launch traced here: 127 us
  waiting for transfers between devices  62.8 us (49%)
  local copies, waits for them, and re-layouts  23.1 us (18%)
  matrix products  15.1 us (12%)
  between operations  14.3 us (11%)
  starting transfers between devices  7.81 us (6%)
  other arithmetic  4.03 us (3%)
    reduce_scatter x1, waiting for transfers between devices, local(): lax.psum_scatter(summed * normalizer, 'pair', scatter_dimension=0, tiled=...  47.8 us
    all_to_all x1, waiting for transfers between devices, local(): lax.all_to_all(row_slab[None], 'tm', split_axis=2, concat_axis=0, tiled=T...  9.27 us
    dot_general x1, matrix products, local(): lax.dot_general(left_side, right_side, (((0,), (0,)), ((), ())), preferre...  8.26 us
    ppermute x3, waiting for transfers between devices, local(): lax.ppermute(sent, 'tm', [(i, (i + step) % devices) for i in range(device...  5.67 us
    dot_general x1, matrix products, local(): jnp.einsum('mjx,jxy->mjy', gathered, factors, precision=lax.Precision.HIG...  4.77 us
    gather x2, local copies, waits for them, and re-layouts, half_product(): picked = green_matrix[0][pair_list]  4.42 us
    all_to_all x1, starting transfers between devices, local(): lax.all_to_all(row_slab[None], 'tm', split_axis=2, concat_axis=0, tiled=T...  4.14 us
    ppermute x3, starting transfers between devices, local(): lax.ppermute(sent, 'tm', [(i, (i + step) % devices) for i in range(device...  3.67 us
  transfers between devices with their start and end apart: 5, of which 4 were waited for; matrix products, arithmetic and copies ran while one was open for 0% of the time, Pallas kernels for 0%

profile of v1, /device:TPU:16, one launch (start us, length us, event | category | flops | bytes accessed | tf_op | source)
XLA Modules:
  0.0 127.1 jit_solution(13330150208264891212)
XLA Ops:
  6.5 0.0 copy-start
  6.5 0.0 reduce-scatter.2.cloned.1.call-start
  7.4 0.8 compare_select_fusion.2
  8.2 1.8 %gather_fusion.1 = bf16[24,64,64]{2,1,0:T(8,128)(2,1)S(1)} fusion(bf16[64,64,64]{2,1,0:T(8,128)(2,1)} %bitcast.61, s32[1024]{0:T(1024)S(1)} %pad_clamp_fusion.2), kind=kCustom, calls=%fused_computation.1 | custom fusion | bytes 393312 | tf_op jit(solution)/shard_map/gather | solution.py:21
  10.0 2.6 %gather_fusion = bf16[24,64,64]{2,1,0:T(8,128)(2,1)} fusion(bf16[64,64,64]{2,1,0:T(8,128)(2,1)} %bitcast.62, s32[1024]{0:T(1024)S(1)} %pad_clamp_fusion.2), kind=kCustom, calls=%fused_computation | custom fusion | bytes 393312 | tf_op jit(solution)/shard_map/gather | solution.py:21
  12.6 0.0 copy-done
  12.6 8.3 %bitcast_multiply_fusion = f32[1024,1024]{1,0:T(8,128)} fusion(f32[24]{0:T(128)S(1)} %compare_convert_fusion, bf16[24,64,64]{2,1,0:T(8,128)(2,1)S(1)} %gather_fusion.1, bf16[24,64,1024]{2,1,0:T(8,128)(2,1)S(1)} %copy-done, bf16[24,64,64]{2,1,0:T(8,128)(2,1)} %gather_fusion), kind=kOutput, calls=%fused_computation.6 | convolution fusion | flops 3631218688 | bytes 7733344 | tf_op jit(solution)/shard_map/dot_general | solution.py:43
  20.9 0.0 copy-start.2
  20.9 0.0 copy-start.1
  20.9 0.0 reduce-scatter.2.cloned.1.call-update
  20.9 0.6 copy-done.2
  21.5 0.1 copy.23
  21.6 0.1 reshape.118
  21.7 0.1 reshape.117
  21.8 47.8 %reduce-scatter.2.cloned.1.call-done = f32[128,1024]{1,0:T(8,128)} async-done(((f32[1024,1024]{1,0:T(8,128)}), f32[128,1024]{1,0:T(8,128)}) %reduce-scatter.2.cloned.1.call-update) | async-done | bytes 524304 | tf_op jit(solution)/shard_map/reduce_scatter | solution.py:46
  69.6 1.9 %copy.24 = f32[1,128,1024]{1,0,2:T(1,128)} copy(f32[1,128,1024]{2,1,0:T(8,128)} %bitcast.59) | data formatting | bytes 1048576 | tf_op jit(solution)/shard_map/broadcast_in_dim | solution.py:50
  71.5 4.1 %all-to-all-start = ((f32[1,128,1024]{1,0,2:T(1,128)}), f32[1,128,1024]{1,0,2:T(1,128)}, u32[]{:S(2)}, u32[]{:S(2)}) async-start(f32[1,128,1024]{1,0,2:T(1,128)} %copy.24), calls=%async_computation.1 | async-start | bytes 1048576 | tf_op jit(solution)/shard_map/all_to_all | solution.py:50
  75.7 9.3 %all-to-all-done = f32[1,128,1024]{1,0,2:T(1,128)} async-done(((f32[1,128,1024]{1,0,2:T(1,128)}), f32[1,128,1024]{1,0,2:T(1,128)}, u32[]{:S(2)}, u32[]{:S(2)}) %all-to-all-start) | async-done | bytes 524320 | tf_op jit(solution)/shard_map/all_to_all | solution.py:50
  85.0 2.0 %copy.31 = f32[1,128,4,256]{3,2,1,0:T(4,128)} copy(f32[1,128,4,256]{1,3,2,0:T(8,128)} %bitcast.5) | data formatting | bytes 1048576 | tf_op jit(solution)/shard_map/all_to_all | solution.py:50
  87.0 0.0 copy-done.1
  87.0 2.0 %fusion.11 = f32[128,256,4]{1,2,0:T(4,128)S(1)} fusion(f32[1,128,4,256]{3,2,1,0:T(4,128)} %copy.31, f32[4,4]{1,0:T(4,128)S(1)} %copy-done.1), kind=kOutput, calls=%fused_computation.17 | convolution fusion | flops 6291456 | bytes 1048640 | tf_op jit(solution)/shard_map/ft,trc->frc/dot_general | solution.py:47
  89.1 0.5 constant_dynamic-slice_fusion.3
  89.5 1.5 %collective-permute-start.2 = (f32[1,128,256]{2,1,0:T(8,128)S(1)}, f32[1,128,256]{2,1,0:T(8,128)S(1)}, u32[]{:S(2)}, u32[]{:S(2)}) collective-permute-start(f32[1,128,256]{2,1,0:T(8,128)S(1)} %bitcast.63), channel_id=1, source_target_pairs={{0,24},{8,0},{16,8},{24,16},{1,25},{9,1},{17,9},{25,17},{2,26},{10... | collective-permute-start | bytes 393224 | tf_op jit(solution)/shard_map/ppermute | solution.py:58
  91.0 1.5 %collective-permute-start.1 = (f32[1,128,256]{2,1,0:T(8,128)S(1)}, f32[1,128,256]{2,1,0:T(8,128)S(1)}, u32[]{:S(2)}, u32[]{:S(2)}) collective-permute-start(f32[1,128,256]{2,1,0:T(8,128)S(1)} %bitcast.64), channel_id=1, source_target_pairs={{0,16},{8,24},{16,0},{24,8},{1,17},{9,25},{17,1},{25,9},{2,18},{10... | collective-permute-start | bytes 393224 | tf_op jit(solution)/shard_map/ppermute | solution.py:58
  92.6 0.7 collective-permute-start
  93.3 2.0 %collective-permute-done.2 = f32[1,128,256]{2,1,0:T(8,128)S(1)} collective-permute-done((f32[1,128,256]{2,1,0:T(8,128)S(1)}, f32[1,128,256]{2,1,0:T(8,128)S(1)}, u32[]{:S(2)}, u32[]{:S(2)}) %collective-permute-start.2) | collective-permute-done | bytes 131104 | tf_op jit(solution)/shard_map/ppermute | solution.py:58
  95.3 3.7 %collective-permute-done.1 = f32[1,128,256]{2,1,0:T(8,128)S(1)} collective-permute-done((f32[1,128,256]{2,1,0:T(8,128)S(1)}, f32[1,128,256]{2,1,0:T(8,128)S(1)}, u32[]{:S(2)}, u32[]{:S(2)}) %collective-permute-start.1) | collective-permute-done | bytes 131104 | tf_op jit(solution)/shard_map/ppermute | solution.py:58
  98.9 0.0 collective-permute-done
  99.0 0.8 maximum_bitcast_fusion
  99.8 2.4 %gather_fusion.2 = f32[4,128,256]{2,1,0:T(8,128)} fusion(f32[4,128,256]{2,1,0:T(8,128)} %maximum_bitcast_fusion, s32[1024]{0:T(1024)S(1)} %pad_clamp_fusion.1), kind=kCustom, calls=%fused_computation.2 | custom fusion | bytes 1048592 | tf_op jit(solution)/shard_map/gather | solution.py:59
  102.2 2.0 %copy.26 = f32[1,128,4,256]{1,3,2,0:T(8,128)} copy(f32[1,128,4,256]{3,1,2,0:T(8,128)} %bitcast.55) | data formatting | bytes 1048576 | tf_op jit(solution)/shard_map/transpose | solution.py:15
  104.2 2.0 %copy.28 = f32[128,8,128]{2,0,1:T(8,128)} copy(f32[128,8,128]{0,2,1:T(8,128)} %bitcast.56) | data formatting | bytes 1048576 | tf_op jit(solution)/shard_map/reshape;reshape | solution.py:65
  106.3 2.8 %gather_fusion.3 = f32[24,128,128]{2,1,0:T(8,128)} fusion(f32[128,8,128]{2,0,1:T(8,128)} %copy.28, s32[1024]{0:T(1024)S(1)} %pad_clamp_fusion), kind=kCustom, calls=%fused_computation.3 | custom fusion | bytes 3145824 | tf_op jit(solution)/shard_map/jit(_take)/gather | solution.py:66
  109.1 4.8 %fusion.6 = f32[24,128,128]{2,1,0:T(8,128)} fusion(f32[24,128,128]{2,1,0:T(8,128)} %bitcast.58, f32[24,128,128]{2,1,0:T(8,128)} %gather_fusion.3, pred[24]{0:T(512)(128)(4,1)S(1)} %compare_and_fusion), kind=kOutput, calls=%fused_computation.11 | convolution fusion | flops 604372992 | bytes 4718616 | tf_op jit(solution)/shard_map/mjx,jxy->mjy/dot_general | solution.py:68
  113.9 2.3 %reduce_sum.9 = f32[128,8,128]{2,0,1:T(8,128)} reduce(f32[128,8,3,128]{3,0,2,1:T(8,128)} %bitcast.54, f32[]{:T(128)} %constant.63.clone.1), dimensions={2}, to_apply=%region_1.2 | reduce | flops 262144 | bytes 2097156 | tf_op jit(solution)/shard_map/reduce_sum | solution.py:69
  116.2 2.0 %copy.29 = f32[128,8,128]{0,2,1:T(8,128)} copy(f32[128,8,128]{2,0,1:T(8,128)} %reduce_sum.9) | data formatting | bytes 1048576 | tf_op jit(solution)/shard_map/reduce_sum | solution.py:69
  118.3 2.0 %copy.30 = f32[1,128,1024]{2,1,0:T(8,128)} copy(f32[1,128,1024]{1,2,0:T(8,128)} %bitcast.57) | data formatting | bytes 1048576 | tf_op jit(solution)/shard_map/reshape | solution.py:70
  (11 shorter events, 0.1 us)
Async XLA Ops:
  6.5 6.1 %copy-start = (bf16[24,64,1024]{2,1,0:T(8,128)(2,1)S(1)}, bf16[24,64,1024]{2,1,0:T(8,128)(2,1)}, u32[]{:S(2)}) copy-start(bf16[24,64,1024]{2,1,0:T(8,128)(2,1)} %param.8) | copy-start | bytes 9437188
  6.5 63.1 %reduce-scatter.2.cloned.1.call-start = ((), (), s32[]{:S(2)}) async-start(), calls=%async_computation.2 | async-start | bytes 4718592 | tf_op jit(solution)/shard_map/reduce_scatter | solution.py:46
  20.9 0.7 copy-start.2
  20.9 66.1 %copy-start.1 = (f32[4,4]{1,0:T(4,128)S(1)}, f32[4,4]{1,0:T(4,128)}, u32[]{:S(2)}) copy-start(f32[4,4]{1,0:T(4,128)} %param.13) | copy-start | bytes 196
  71.5 13.4 %all-to-all-start = ((f32[1,128,1024]{1,0,2:T(1,128)}), f32[1,128,1024]{1,0,2:T(1,128)}, u32[]{:S(2)}, u32[]{:S(2)}) async-start(f32[1,128,1024]{1,0,2:T(1,128)} %copy.24), calls=%async_computation.1 | async-start | bytes 1048576 | tf_op jit(solution)/shard_map/all_to_all | solution.py:50
  89.5 5.7 %collective-permute-start.2 = (f32[1,128,256]{2,1,0:T(8,128)S(1)}, f32[1,128,256]{2,1,0:T(8,128)S(1)}, u32[]{:S(2)}, u32[]{:S(2)}) collective-permute-start(f32[1,128,256]{2,1,0:T(8,128)S(1)} %bitcast.63), channel_id=1, source_target_pairs={{0,24},{8,0},{16,8},{24,16},{1,25},{9,1},{17,9},{25,17},{2,26},{10... | collective-permute-start | bytes 393224 | tf_op jit(solution)/shard_map/ppermute | solution.py:58
  91.0 7.9 %collective-permute-start.1 = (f32[1,128,256]{2,1,0:T(8,128)S(1)}, f32[1,128,256]{2,1,0:T(8,128)S(1)}, u32[]{:S(2)}, u32[]{:S(2)}) collective-permute-start(f32[1,128,256]{2,1,0:T(8,128)S(1)} %bitcast.64), channel_id=1, source_target_pairs={{0,16},{8,24},{16,0},{24,8},{1,17},{9,25},{17,1},{25,9},{2,18},{10... | collective-permute-start | bytes 393224 | tf_op jit(solution)/shard_map/ppermute | solution.py:58
  92.6 6.4 %collective-permute-start = (f32[1,128,256]{2,1,0:T(8,128)S(1)}, f32[1,128,256]{2,1,0:T(8,128)S(1)}, u32[]{:S(2)}, u32[]{:S(2)}) collective-permute-start(f32[1,128,256]{2,1,0:T(8,128)S(1)} %bitcast.65), channel_id=1, source_target_pairs={{0,8},{8,16},{16,24},{24,0},{1,9},{9,17},{17,25},{25,1},{2,10},{10... | collective-permute-start | bytes 393224 | tf_op jit(solution)/shard_map/ppermute | solution.py:58
Sparse Core Ops, SparseCore 0:
  21.0 48.5 reduce-scatter.1
